TPU v7x, 32 devices: a whole 2x2x4 slice. The times are simulated.
32 devices in a mesh: tok: 16 (over z, y, x), col: 2 (over core).
Axes of the slice: x: 2, y: 2, z: 4, core: 2. Of those that a mesh axis runs over, the one named last changes fastest.
Arguments:
- activations: bfloat16 [512, 6144], P('tok', 'col'), may hold values from -61 to 61
- block_slot: int32 [6], replicated, may hold values from 0 to 5, each once
- slot_tile: int32 [32], replicated, may hold values from 0 to 31, each once
Outputs:
- gram_tiles: float32 [32, 1024, 1024], P(('tok', 'col'))
- col_mean: float32 [6144], P('col')
- col_var: float32 [6144], P('col')
Inputs may be any that keep to these rules, and one draw needn't show every extreme that they name: `block_slot`: each stored position once. `slot_tile`: each value once.
All inputs are finite; a program needn't handle non-finite values.
Results may differ from a plain program's by a relative error of at most 0.0003.
Values may be sent and summed in bfloat16 or wider, within the bound.
No kernel may reach another device: no remote copies, remote signals or barrier semaphores. Data moves between devices by JAX's collectives and lax.ppermute only.
A program may use at most 64 MiB of HBM per device.

v0:
```python
import jax
import jax.numpy as jnp
import numpy as np
from jax import lax
from jax.sharding import PartitionSpec as P

BS = 1024


def on_device(activations, block_slot, slot_tile):
    n_tok = lax.axis_size("tok")
    n_col = lax.axis_size("col")
    tok_dev = activations.shape[0]
    total_tokens = tok_dev * n_tok
    col_index = lax.axis_index("col")
    values = activations.astype(jnp.float32)
    col_sum = lax.psum(jnp.sum(values, axis=0), "tok")
    col_mean = col_sum / total_tokens
    squares = lax.psum(jnp.sum((values - col_mean) ** 2, axis=0), "tok")
    col_var = squares / total_tokens
    gathered = lax.all_gather(activations, "col", axis=1, tiled=True)
    block_count = gathered.shape[1] // BS
    pair_count = block_count * (block_count + 1) // 2
    rows_np, cols_np = np.triu_indices(block_count)
    row_table = jnp.asarray(rows_np.astype(np.int32))
    col_table = jnp.asarray(cols_np.astype(np.int32))
    slot_grid = slot_tile.reshape(n_tok, n_col)
    peer_tiles = lax.dynamic_index_in_dim(slot_grid, col_index, 1, keepdims=False)
    clamped = jnp.where(peer_tiles < pair_count, peer_tiles, 0)
    first_slot = block_slot[row_table[clamped]]
    second_slot = block_slot[col_table[clamped]]
    blocks = gathered.reshape(tok_dev, block_count, BS)
    picked = jnp.take(blocks, jnp.stack([first_slot, second_slot], axis=1), axis=1)
    outgoing = picked.transpose(1, 0, 2, 3).reshape(n_tok, tok_dev, 2 * BS)
    arrived = lax.all_to_all(outgoing, "tok", split_axis=0, concat_axis=0, tiled=True)
    arrived = arrived.reshape(n_tok * tok_dev, 2 * BS)
    own_slot = lax.axis_index("tok") * n_col + col_index
    own_tile = lax.dynamic_index_in_dim(slot_tile, own_slot, 0, keepdims=False)
    left_block = arrived[:, :BS]
    right_block = arrived[:, BS:]
    product = (
        lax.dot_general(
            left_block, right_block, (((0,), (0,)), ((), ())), preferred_element_type=jnp.float32
        )
        / total_tokens
    )
    product = jnp.where(own_tile < pair_count, product, jnp.zeros_like(product))
    return (product[None], col_mean, col_var)


def solution(mesh):
    return jax.shard_map(
        on_device,
        mesh=mesh,
        in_specs=(P("tok", "col"), P(), P()),
        out_specs=(P(("tok", "col"), None, None), P("col"), P("col")),
        check_vma=False,
    )
```

profile of v0, /device:TPU:0, one launch (start us, length us, event | category | flops | bytes accessed | tf_op | source)
XLA Modules:
  0.0 200.0 jit_solution(13010305735175130137)
XLA Ops:
  0.6 0.0 copy-start
  0.6 0.0 copy-start.1
  0.7 0.8 reshape.144
  1.4 0.2 fusion.4
  1.6 1.3 gather_fusion
  3.0 0.1 copy.16
  3.0 0.1 fusion.5
  3.2 1.3 gather_fusion.2
  4.5 0.1 copy.19
  4.6 0.1 fusion.6
  4.7 0.0 copy-done
  4.7 0.7 gather_fusion.1
  5.4 0.7 gather_fusion.3
  6.1 0.1 copy.23
  6.1 0.1 reshape.182
  6.3 0.0 copy-done.1
  6.3 2.2 %all_gather.3 = bf16[32,6144]{1,0:T(8,128)(2,1)S(1)} all-gather(bf16[32,3072]{1,0:T(8,128)(2,1)S(1)} %copy-done.1), channel_id=1, replica_groups=mesh['tok'=16,'col'=2] {'col'}, dimensions={1}, use_global_device_ids=true | all-gather | bytes 589824 | tf_op jit(solution)/shard_map/all_gather | solution.py:21
  8.5 0.1 copy.22
  8.6 0.7 gather_fusion.4
  9.3 0.3 select_bitcast_fusion.1
  9.5 1.5 copy.27
  11.1 0.0 copy-start.3
  11.1 8.4 %all-to-all-start = ((bf16[16,32,2048]{2,1,0:T(8,128)(2,1)}), bf16[16,32,2048]{2,1,0:T(8,128)(2,1)S(1)}, u32[]{:S(2)}, u32[]{:S(2)}) async-start(bf16[16,32,2048]{2,1,0:T(8,128)(2,1)} %bitcast.14), calls=%async_computation | async-start | bytes 4194304 | tf_op jit(solution)/shard_map/all_to_all | solution.py:35
  19.5 0.0 copy-done.3
  19.5 0.6 dynamic_slice.8
  20.8 103.5 %psum.14 = f32[3072]{0:T(1024)S(1)} all-reduce(f32[3072]{0:T(1024)S(1)} %convert_reduce_fusion), channel_id=1, replica_groups=mesh['tok'=16,'col'=2] {'tok'}, use_global_device_ids=true, to_apply=%region_1.0 | all-reduce | flops 3072 | bytes 24576 | tf_op jit(solution)/shard_map/psum | solution.py:17
  124.3 0.1 fusion.3
  124.3 71.7 %psum.15 = f32[3072]{0:T(1024)S(1)} all-reduce(f32[3072]{0:T(1024)S(1)} %fusion.3), channel_id=1, replica_groups=mesh['tok'=16,'col'=2] {'tok'}, use_global_device_ids=true, to_apply=%region_3.0 | all-reduce | flops 3072 | bytes 24576 | tf_op jit(solution)/shard_map/psum | solution.py:19
  196.1 0.6 broadcast_multiply_fusion
  196.7 0.0 all-to-all-done
  196.7 3.3 %select_bitcast_fusion = f32[1,1024,1024]{2,1,0:T(8,128)} fusion(pred[]{:T(512)} %bitcast, bf16[512,2048]{1,0:T(8,128)(2,1)S(1)} %bitcast.23), kind=kOutput, calls=%fused_computation.5 | convolution fusion | flops 1075838976 | bytes 6291457 | tf_op jit(solution)/shard_map/dot_general | solution.py:42
  200.0 0.0 copy-done.2
  (10 shorter events, 0.1 us)
Async XLA Ops:
  0.6 4.1 %copy-start = (s32[6]{0:T(128)S(1)}, s32[6]{0:T(128)}, u32[]{:S(2)}) copy-start(s32[6]{0:T(128)} %param.6) | copy-start | bytes 76
  0.6 5.6 %copy-start.1 = (bf16[32,3072]{1,0:T(8,128)(2,1)S(1)}, bf16[32,3072]{1,0:T(8,128)(2,1)}, u32[]{:S(2)}) copy-start(bf16[32,3072]{1,0:T(8,128)(2,1)} %param.5) | copy-start | bytes 589828
  11.1 8.4 %copy-start.3 = (s32[32]{0:T(128)S(1)}, s32[32]{0:T(128)}, u32[]{:S(2)}) copy-start(s32[32]{0:T(128)} %param.7) | copy-start | bytes 388
  11.1 185.6 %all-to-all-start = ((bf16[16,32,2048]{2,1,0:T(8,128)(2,1)}), bf16[16,32,2048]{2,1,0:T(8,128)(2,1)S(1)}, u32[]{:S(2)}, u32[]{:S(2)}) async-start(bf16[16,32,2048]{2,1,0:T(8,128)(2,1)} %bitcast.14), calls=%async_computation | async-start | bytes 4194304 | tf_op jit(solution)/shard_map/all_to_all | solution.py:35
  124.3 75.7 %copy-start.2 = (f32[3072]{0:T(1024)}, f32[3072]{0:T(1024)S(1)}, u32[]{:S(2)}) copy-start(f32[3072]{0:T(1024)S(1)} %broadcast_multiply_fusion.1) | copy-start | bytes 36868
where the time goes:
time: 200 us
  blocking collectives  177 us (88%)
  starting transfers between devices  8.36 us (4%)
  local copies, waits for them, and re-layouts  8.04 us (4%)
  matrix products  3.31 us (2%)
    psum x1, blocking collectives, on_device(): col_sum = lax.psum(jnp.sum(values, axis=0), 'tok')  103 us
    psum x1, blocking collectives, on_device(): squares = lax.psum(jnp.sum((values - col_mean) ** 2, axis=0), 'tok')  71.7 us
    all_to_all x1, starting transfers between devices, on_device(): lax.all_to_all(outgoing, 'tok', split_axis=0, concat_axis=0, tiled=True)  8.36 us
  transfers between devices with their start and end apart: 1, of which 0 were waited for; matrix products, arithmetic and copies ran while one was open for 1% of the time, Pallas kernels for 0%

commit v1 on v0

--- a/solution.py
+++ b/solution.py
@@ -14,7 +14,13 @@
     total_tokens = tok_dev * n_tok
     col_index = lax.axis_index("col")
     values = activations.astype(jnp.float32)
-    col_sum = lax.psum(jnp.sum(values, axis=0), "tok")
+
+    def stocks_cut(inp, a_name):
+        tmp = jax.lax.all_gather(inp, axis_name=a_name)
+        fresh = jnp.sum(tmp, 0)
+        return fresh
+
+    col_sum = stocks_cut(jnp.sum(values, axis=0), "tok")
     col_mean = col_sum / total_tokens
     squares = lax.psum(jnp.sum((values - col_mean) ** 2, axis=0), "tok")
     col_var = squares / total_tokens

time: 200 us -> 170 us (0.85)
  blocking collectives: 177 us -> 147 us
    psum x1 -> x0, blocking collectives: 103 us -> none  [on_device(): col_sum = lax.psum(jnp.sum(values, axis=0), 'tok')]
    all_gather x0 -> x1, blocking collectives: none -> 69.7 us  [stocks_cut(): tmp = jax.lax.all_gather(inp, axis_name=a_name)]
    psum x1, blocking collectives: 71.7 us -> 75.2 us  [on_device(): squares = lax.psum(jnp.sum((values - col_mean) ** 2, axis=0), 'tok')]
where the time goes in v1:
time: 170 us
  blocking collectives  147 us (86%)
  starting transfers between devices  8.36 us (5%)
  local copies, waits for them, and re-layouts  8.08 us (5%)
  matrix products  3.31 us (2%)
    psum x1, blocking collectives, on_device(): squares = lax.psum(jnp.sum((values - col_mean) ** 2, axis=0), 'tok')  75.2 us
    all_gather x1, blocking collectives, stocks_cut(): tmp = jax.lax.all_gather(inp, axis_name=a_name)  69.7 us
    all_to_all x1, starting transfers between devices, on_device(): lax.all_to_all(outgoing, 'tok', split_axis=0, concat_axis=0, tiled=True)  8.36 us
  transfers between devices with their start and end apart: 1, of which 0 were waited for; matrix products, arithmetic and copies ran while one was open for 1% of the time, Pallas kernels for 0%

profile of v1, /device:TPU:0, one launch (start us, length us, event | category | flops | bytes accessed | tf_op | source)
XLA Modules:
  0.0 169.8 jit_solution(9433689580438644498)
XLA Ops:
  0.6 0.0 copy-start
  0.6 0.0 copy-start.1
  0.7 0.8 reshape.146
  1.4 0.2 fusion.4
  1.6 1.3 gather_fusion
  3.0 0.1 copy.36
  3.0 0.1 fusion.5
  3.2 1.3 gather_fusion.2
  4.5 0.1 copy.39
  4.6 0.1 fusion.6
  4.7 0.0 copy-done
  4.7 0.7 gather_fusion.1
  5.4 0.7 gather_fusion.3
  6.1 0.1 copy.43
  6.1 0.1 reshape.184
  6.3 0.0 copy-done.1
  6.3 2.2 %all_gather.9 = bf16[32,6144]{1,0:T(8,128)(2,1)S(1)} all-gather(bf16[32,3072]{1,0:T(8,128)(2,1)S(1)} %copy-done.1), channel_id=1, replica_groups=mesh['tok'=16,'col'=2] {'col'}, dimensions={1}, use_global_device_ids=true | all-gather | bytes 589824 | tf_op jit(solution)/shard_map/all_gather | solution.py:27
  8.5 0.1 copy.42
  8.6 0.7 gather_fusion.4
  9.3 0.3 select_bitcast_fusion.1
  9.5 1.5 copy.47
  11.1 8.4 %all-to-all-start = ((bf16[16,32,2048]{2,1,0:T(8,128)(2,1)}), bf16[16,32,2048]{2,1,0:T(8,128)(2,1)S(1)}, u32[]{:S(2)}, u32[]{:S(2)}) async-start(bf16[16,32,2048]{2,1,0:T(8,128)(2,1)} %bitcast.14), calls=%async_computation | async-start | bytes 4194304 | tf_op jit(solution)/shard_map/all_to_all | solution.py:41
  19.5 0.0 copy-done.3
  19.5 0.6 dynamic_slice.8
  20.1 69.7 %all-gather = f32[49152]{0:T(1024)S(1)} all-gather(f32[3072]{0:T(1024)S(1)} %convert_reduce_fusion), channel_id=2, replica_groups=mesh['tok'=16,'col'=2] {'tok'}, dimensions={0}, use_global_device_ids=true | all-gather | bytes 208896 | tf_op jit(solution)/shard_map/all_gather | solution.py:19
  90.6 0.0 copy-start.2
  90.6 0.1 fusion.3
  90.7 75.2 %psum.7 = f32[3072]{0:T(1024)S(1)} all-reduce(f32[3072]{0:T(1024)S(1)} %fusion.3), channel_id=1, replica_groups=mesh['tok'=16,'col'=2] {'tok'}, use_global_device_ids=true, to_apply=%region_3.0 | all-reduce | flops 3072 | bytes 24576 | tf_op jit(solution)/shard_map/psum | solution.py:25
  165.8 0.6 broadcast_multiply_fusion
  166.4 0.0 all-to-all-done
  166.4 3.3 %select_bitcast_fusion = f32[1,1024,1024]{2,1,0:T(8,128)} fusion(pred[]{:T(512)} %bitcast, bf16[512,2048]{1,0:T(8,128)(2,1)S(1)} %bitcast.23), kind=kOutput, calls=%fused_computation.5 | convolution fusion | flops 1075838976 | bytes 6291457 | tf_op jit(solution)/shard_map/dot_general | solution.py:48
  169.8 0.0 copy-done.2
  (12 shorter events, 0.2 us)
Async XLA Ops:
  0.6 4.1 %copy-start = (s32[6]{0:T(128)S(1)}, s32[6]{0:T(128)}, u32[]{:S(2)}) copy-start(s32[6]{0:T(128)} %param.6) | copy-start | bytes 76
  0.6 5.6 %copy-start.1 = (bf16[32,3072]{1,0:T(8,128)(2,1)S(1)}, bf16[32,3072]{1,0:T(8,128)(2,1)}, u32[]{:S(2)}) copy-start(bf16[32,3072]{1,0:T(8,128)(2,1)} %param.5) | copy-start | bytes 589828
  11.1 8.4 %copy-start.3 = (s32[32]{0:T(128)S(1)}, s32[32]{0:T(128)}, u32[]{:S(2)}) copy-start(s32[32]{0:T(128)} %param.7) | copy-start | bytes 388
  11.1 155.4 %all-to-all-start = ((bf16[16,32,2048]{2,1,0:T(8,128)(2,1)}), bf16[16,32,2048]{2,1,0:T(8,128)(2,1)S(1)}, u32[]{:S(2)}, u32[]{:S(2)}) async-start(bf16[16,32,2048]{2,1,0:T(8,128)(2,1)} %bitcast.14), calls=%async_computation | async-start | bytes 4194304 | tf_op jit(solution)/shard_map/all_to_all | solution.py:41
  90.6 79.2 %copy-start.2 = (f32[3072]{0:T(1024)}, f32[3072]{0:T(1024)S(1)}, u32[]{:S(2)}) copy-start(f32[3072]{0:T(1024)S(1)} %broadcast_multiply_fusion.1) | copy-start | bytes 36868
